TPU v7x, 256 devices: a whole 4x4x8 slice. The times are simulated.
256 devices in a mesh: pts: 8 (over x, core), rows: 32 (over z, y).
Axes of the slice: x: 4, y: 4, z: 8, core: 2. Of those that a mesh axis runs over, the one named last changes fastest.
Arguments:
- solutions: bfloat16 [16, 262144, 128], P('pts', 'rows'), may hold values from -6 to 6
- probe: bfloat16 [64, 262144], P(None, 'rows'), may hold values from -0.01171875 to 0.01171875
- left_factor: float32 [256, 256], replicated, may hold values from -0.375 to 0.375
- singular: float32 [256], replicated, may hold values from 1 to 13.8, as said below
- right_factor: float32 [256, 256], replicated, may hold values from -0.375 to 0.375
- reduced_adjoint: float32 [256, 256], replicated, may hold values from -6 to 6
Outputs:
- solution_adjoint: bfloat16 [16, 262144, 128], P('pts', 'rows')
Inputs may be any that keep to these rules, and one draw needn't show every extreme that they name: `singular`: rising, each value at least 0.03 above the one before.
All inputs are finite; a program needn't handle non-finite values.
Results may differ from a plain program's by a relative error of at most 0.0049.
Values sent between devices are 32-bit elements; how exact they have to be, the bound alone decides.
A program may use at most 64 MiB of HBM per device.

v0:
```python
import math
import jax
import jax.numpy as jnp
from jax import lax
from jax.sharding import PartitionSpec as P

L = 64
K = 4


def coefficients(first, count, total, orders):
    theta = math.pi * (first + jnp.arange(count, dtype=jnp.float32) + 0.5) / total
    angle = theta[:, None] * orders[None, :]
    return (jnp.cos(angle) / total, jnp.sin(angle) / total)


def matmul(first, second):
    return jnp.dot(
        first, second, precision=lax.Precision.HIGHEST, preferred_element_type=jnp.float32
    )


def svd_back(hankel, left, sing, right, adjoint):
    quot = matmul(left.T, hankel)
    prod_right = matmul(hankel, right)
    zmat = matmul(quot, right)
    zbar = adjoint / sing[None, :]
    sbar = -jnp.sum(adjoint * zmat, axis=0) / (sing * sing)
    ubar = matmul(prod_right, zbar.T)
    wbar = matmul(quot.T, zbar)
    left_term = matmul(left.T, ubar)
    right_term = matmul(right.T, wbar)
    square = sing * sing
    eye_mask = jnp.eye(sing.shape[0], dtype=bool)
    recip = jnp.where(
        eye_mask, 0.0, 1.0 / jnp.where(eye_mask, 1.0, square[None, :] - square[:, None])
    )
    core = (
        recip * (left_term - left_term.T) * sing[None, :]
        + jnp.diag(sbar)
        + sing[:, None] * (recip * (right_term - right_term.T))
    )
    return (core, zbar)


def build_hankel(moments):
    return jnp.concatenate(
        [jnp.concatenate([moments[i + j] for j in range(K)], axis=1) for i in range(K)], axis=0
    )


def per_device(solutions, probe, left_factor, singular, right_factor, reduced_adjoint):
    hi = lax.Precision.HIGHEST
    point_count = solutions.shape[0]
    total = point_count * lax.axis_size("pts")
    first = (lax.axis_index("pts") * point_count).astype(jnp.float32)
    orders = jnp.arange(1, 2 * K + 1, dtype=jnp.float32)
    cos_t, sin_t = coefficients(first, point_count, total, orders)
    gram = jnp.einsum("ln,pnc->plc", probe, solutions, preferred_element_type=jnp.float32)
    moments = lax.psum(
        jnp.einsum("pk,plc->klc", cos_t[:, 1:], gram[:, :, :L], precision=hi)
        - jnp.einsum("pk,plc->klc", sin_t[:, 1:], gram[:, :, L:], precision=hi),
        ("pts", "rows"),
    )
    hankel = build_hankel(moments)
    core, zbar = svd_back(hankel, left_factor, singular, right_factor, reduced_adjoint)
    first_bar = matmul(matmul(left_factor, core), right_factor.T)
    second_bar = matmul(matmul(left_factor, zbar), right_factor.T)
    blocks = [jnp.zeros((L, L), jnp.float32) for k in range(2 * K)]
    for i in range(K):
        for j in range(K):
            blocks[i + j] = blocks[i + j] + first_bar[i * L : (i + 1) * L, j * L : (j + 1) * L]
            blocks[i + j + 1] = (
                blocks[i + j + 1] + second_bar[i * L : (i + 1) * L, j * L : (j + 1) * L]
            )
    moment_adjoint = jnp.stack(blocks)
    weights = jnp.concatenate(
        [
            jnp.einsum("pk,klc->plc", cos_t, moment_adjoint, precision=hi),
            -jnp.einsum("pk,klc->plc", sin_t, moment_adjoint, precision=hi),
        ],
        axis=2,
    ).astype(jnp.bfloat16)
    result = jnp.einsum("ln,plc->pnc", probe, weights, preferred_element_type=jnp.float32)
    return result.astype(jnp.bfloat16)


def solution(mesh):
    in_specs = (P("pts", "rows", None), P(None, "rows"), P(), P(), P(), P())
    out_specs = P("pts", "rows", None)
    return jax.shard_map(
        per_device, mesh=mesh, in_specs=in_specs, out_specs=out_specs, check_vma=False
    )
```

profile of v0, /device:TPU:2, one launch (start us, length us, event | category | flops | bytes accessed | tf_op | source)
XLA Modules:
  0.0 296.1 jit_solution(6354948563807823471)
XLA Ops:
  6.5 0.0 copy-start
  6.5 0.0 copy-start.4
  6.5 0.0 copy-start.3
  6.5 0.0 copy-start.2
  6.5 0.0 copy-start.1
  6.5 0.0 all-reduce.2.cloned.1.call-start
  6.6 1.1 copy-done
  7.8 3.0 %convolution_bitcast_fusion = f32[2,64,128]{2,1,0:T(8,128)S(1)} fusion(bf16[2,8192,128]{2,1,0:T(8,128)(2,1)} %param.6, bf16[64,8192]{1,0:T(8,128)(2,1)S(1)} %copy-done), kind=kOutput, calls=%fused_computation.5 | convolution fusion | flops 268435456 | bytes 5308416 | tf_op jit(solution)/shard_map/ln,pnc->plc/dot_general | solution.py:59
  10.7 0.1 fusion.69
  10.8 0.1 fusion.51
  10.9 0.5 fusion.31
  11.5 1.2 convolution_subtract_fusion
  12.7 0.0 all-reduce.2.cloned.1.call-update
  12.7 0.0 copy-done.4
  12.7 0.0 copy-done.3
  12.7 0.0 copy-done.2
  12.7 0.6 fusion.63
  13.3 0.0 copy-done.1
  13.3 0.6 fusion.73
  13.9 256.3 %all-reduce.2.cloned.1.call-done = f32[7,64,64]{2,0,1:T(8,128)} async-done(((f32[7,64,64]{2,0,1:T(8,128)}), f32[7,64,64]{2,0,1:T(8,128)}) %all-reduce.2.cloned.1.call-update) | async-done | bytes 114704 | tf_op jit(solution)/shard_map/psum | solution.py:60
  270.3 2.1 fusion.68
  272.4 0.7 fusion.66
  273.1 0.6 fusion.1
  273.7 0.4 fusion.64
  274.1 0.4 fusion.67
  274.6 0.6 fusion.71
  275.2 0.4 fusion.65
  275.6 0.6 fusion.70
  276.2 0.1 copy.15
  276.4 0.1 copy.16
  276.5 0.7 fusion.7
  277.3 0.6 fusion.72
  277.9 0.1 fusion.45
  277.9 0.1 fusion.43
  278.0 0.1 fusion.41
  278.1 0.1 fusion.39
  278.2 0.1 fusion.37
  278.3 0.1 fusion.35
  278.4 0.1 fusion.33
  278.5 0.5 fusion.20
  279.0 0.5 fusion.18
  279.6 3.3 %fusion = bf16[2,8192,128]{1,2,0:T(8,128)(2,1)} fusion(bf16[64,8192]{1,0:T(8,128)(2,1)S(1)} %copy-done, bf16[2,64,64]{2,1,0:T(8,128)(2,1)S(1)} %fusion.29, bf16[2,64,64]{2,1,0:T(8,128)(2,1)S(1)} %copy.39), kind=kOutput, calls=%fused_computation.1 | convolution fusion | flops 270598144 | bytes 5275648 | tf_op jit(solution)/shard_map/ln,plc->pnc/dot_general | solution.py:84
  282.9 6.3 %copy.17 = bf16[2,8192,128]{2,1,0:T(8,128)(2,1)} copy(bf16[2,8192,128]{1,2,0:T(8,128)(2,1)} %fusion) | data formatting | bytes 8388608 | tf_op jit(solution)/shard_map/convert_element_type | solution.py:85
  (6 shorter events, 0.0 us)
Async XLA Ops:
  6.5 1.2 copy-start
  6.5 6.2 %copy-start.4 = (f32[256]{0:T(256)S(1)}, f32[256]{0:T(256)}, u32[]{:S(2)}) copy-start(f32[256]{0:T(256)} %param.9) | copy-start | bytes 3076
  6.5 6.2 %copy-start.3 = (f32[256,256]{1,0:T(8,128)S(1)}, f32[256,256]{1,0:T(8,128)}, u32[]{:S(2)}) copy-start(f32[256,256]{1,0:T(8,128)} %param.11) | copy-start | bytes 786436
  6.5 6.2 %copy-start.2 = (f32[256,256]{1,0:T(8,128)S(1)}, f32[256,256]{1,0:T(8,128)}, u32[]{:S(2)}) copy-start(f32[256,256]{1,0:T(8,128)} %param.8) | copy-start | bytes 786436
  6.5 6.8 %copy-start.1 = (f32[256,256]{1,0:T(8,128)S(1)}, f32[256,256]{1,0:T(8,128)}, u32[]{:S(2)}) copy-start(f32[256,256]{1,0:T(8,128)} %param.10) | copy-start | bytes 786436
  6.5 263.7 %all-reduce.2.cloned.1.call-start = ((), (), s32[]{:S(2)}) async-start(), calls=%async_computation | async-start | bytes 524288 | tf_op jit(solution)/shard_map/psum | solution.py:60
Sparse Core Ops, SparseCore 0:
  12.8 257.4 all-reduce.1
where the time goes:
time: 296 us
  waiting for transfers between devices  256 us (86%)
  matrix products  15.4 us (5%)
  between operations  13.7 us (5%)
  local copies, waits for them, and re-layouts  9.97 us (3%)
    psum x1, waiting for transfers between devices, per_device(): lax.psum(jnp.einsum('pk,plc->klc', cos_t[:, 1:], gram[:, :, :L], precisio...  256 us
    dot_general x11, matrix products, matmul(): jnp.dot(first, second, precision=lax.Precision.HIGHEST, preferred_element...  6.33 us
    convert_element_type x1, local copies, waits for them, and re-layouts, per_device(): return result.astype(jnp.bfloat16)  6.31 us
  transfers between devices with their start and end apart: 1, of which 1 were waited for; matrix products, arithmetic and copies ran while one was open for 0% of the time, Pallas kernels for 0%

commit v1 on v0

--- a/solution.py
+++ b/solution.py
@@ -58,9 +58,12 @@
     cos_t, sin_t = coefficients(first, point_count, total, orders)
     gram = jnp.einsum("ln,pnc->plc", probe, solutions, preferred_element_type=jnp.float32)
     moments = lax.psum(
-        jnp.einsum("pk,plc->klc", cos_t[:, 1:], gram[:, :, :L], precision=hi)
-        - jnp.einsum("pk,plc->klc", sin_t[:, 1:], gram[:, :, L:], precision=hi),
-        ("pts", "rows"),
+        lax.psum(
+            jnp.einsum("pk,plc->klc", cos_t[:, 1:], gram[:, :, :L], precision=hi)
+            - jnp.einsum("pk,plc->klc", sin_t[:, 1:], gram[:, :, L:], precision=hi),
+            "rows",
+        ),
+        "pts",
     )
     hankel = build_hankel(moments)
     core, zbar = svd_back(hankel, left_factor, singular, right_factor, reduced_adjoint)

time: 296 us -> 252 us (0.85)
  waiting for transfers between devices: 256 us -> 210 us
    psum x1, waiting for transfers between devices: 256 us -> 148 us  [per_device(): lax.psum(jnp.einsum('pk,plc->klc', cos_t[:, 1:], gram[:, :, :L], precisio...]
    psum x0 -> x1, waiting for transfers between devices: none -> 61.8 us  [per_device(): lax.psum(lax.psum(jnp.einsum('pk,plc->klc', cos_t[:, 1:], gram[:, :, :L],...]
  transfers between devices with their start and end apart: 1 -> 2, of which waited for: 1 -> 2; matrix products, arithmetic and copies ran while one was open for 0% -> 0% of each run, Pallas kernels for 0% -> 0%
where the time goes in v1:
time: 252 us; the launch traced here: 250 us
  waiting for transfers between devices  210 us (83%)
  matrix products  15.4 us (6%)
  between operations  13.7 us (5%)
  local copies, waits for them, and re-layouts  10.1 us (4%)
    psum x1, waiting for transfers between devices, per_device(): lax.psum(jnp.einsum('pk,plc->klc', cos_t[:, 1:], gram[:, :, :L], precisio...  148 us
    psum x1, waiting for transfers between devices, per_device(): lax.psum(lax.psum(jnp.einsum('pk,plc->klc', cos_t[:, 1:], gram[:, :, :L],...  61.8 us
    dot_general x11, matrix products, matmul(): jnp.dot(first, second, precision=lax.Precision.HIGHEST, preferred_element...  6.32 us
    convert_element_type x1, local copies, waits for them, and re-layouts, per_device(): return result.astype(jnp.bfloat16)  6.31 us
  transfers between devices with their start and end apart: 2, of which 2 were waited for; matrix products, arithmetic and copies ran while one was open for 0% of the time, Pallas kernels for 0%

profile of v1, /device:TPU:2, one launch (start us, length us, event | category | flops | bytes accessed | tf_op | source)
XLA Modules:
  0.0 249.9 jit_solution(16861982245677817676)
XLA Ops:
  6.5 0.0 copy-start
  6.5 0.0 copy-start.4
  6.5 0.0 copy-start.3
  6.5 0.0 copy-start.2
  6.5 0.0 copy-start.1
  6.5 0.0 all-reduce.3.cloned.1.call-start
  6.6 1.1 copy-done
  7.8 3.0 %convolution_bitcast_fusion = f32[2,64,128]{2,1,0:T(8,128)S(1)} fusion(bf16[2,8192,128]{2,1,0:T(8,128)(2,1)} %param.6, bf16[64,8192]{1,0:T(8,128)(2,1)S(1)} %copy-done), kind=kOutput, calls=%fused_computation.5 | convolution fusion | flops 268435456 | bytes 5308416 | tf_op jit(solution)/shard_map/ln,pnc->plc/dot_general | solution.py:59
  10.7 0.1 fusion.69
  10.8 0.1 fusion.51
  10.9 0.5 fusion.31
  11.5 1.2 convolution_subtract_fusion
  12.7 0.0 all-reduce.3.cloned.1.call-update
  12.7 0.0 all-reduce.5.cloned.1.call-start
  12.7 0.0 copy-done.4
  12.8 0.0 copy-done.3
  12.8 0.0 copy-done.2
  12.8 0.6 fusion.63
  13.4 148.2 %all-reduce.3.cloned.1.call-done = f32[7,64,64]{2,0,1:T(8,128)} async-done(((f32[7,64,64]{2,0,1:T(8,128)}), f32[7,64,64]{2,0,1:T(8,128)}) %all-reduce.3.cloned.1.call-update) | async-done | bytes 114704 | tf_op jit(solution)/shard_map/psum | solution.py:61
  161.5 0.0 all-reduce.5.cloned.1.call-update
  161.6 0.0 copy-done.1
  161.6 0.6 fusion.73
  162.2 61.8 %all-reduce.5.cloned.1.call-done = f32[7,64,64]{2,0,1:T(8,128)} async-done(((f32[7,64,64]{2,0,1:T(8,128)}), f32[7,64,64]{2,0,1:T(8,128)}) %all-reduce.5.cloned.1.call-update) | async-done | bytes 114704 | tf_op jit(solution)/shard_map/psum | solution.py:60
  224.0 2.2 fusion.68
  226.2 0.7 fusion.66
  226.9 0.6 fusion.1
  227.5 0.4 fusion.64
  227.9 0.4 fusion.67
  228.4 0.6 fusion.71
  229.0 0.4 fusion.65
  229.4 0.6 fusion.70
  230.0 0.1 copy.15
  230.2 0.1 copy.16
  230.3 0.7 fusion.7
  231.0 0.6 fusion.72
  231.7 0.1 fusion.45
  231.7 0.1 fusion.43
  231.8 0.1 fusion.41
  231.9 0.1 fusion.39
  232.0 0.1 fusion.37
  232.1 0.1 fusion.35
  232.2 0.1 fusion.33
  232.3 0.5 fusion.20
  232.8 0.5 fusion.18
  233.4 3.3 %fusion = bf16[2,8192,128]{1,2,0:T(8,128)(2,1)} fusion(bf16[64,8192]{1,0:T(8,128)(2,1)S(1)} %copy-done, bf16[2,64,64]{2,1,0:T(8,128)(2,1)S(1)} %fusion.29, bf16[2,64,64]{2,1,0:T(8,128)(2,1)S(1)} %copy.39), kind=kOutput, calls=%fused_computation.1 | convolution fusion | flops 270598144 | bytes 5275648 | tf_op jit(solution)/shard_map/ln,plc->pnc/dot_general | solution.py:87
  236.7 6.3 %copy.17 = bf16[2,8192,128]{2,1,0:T(8,128)(2,1)} copy(bf16[2,8192,128]{1,2,0:T(8,128)(2,1)} %fusion) | data formatting | bytes 8388608 | tf_op jit(solution)/shard_map/convert_element_type | solution.py:88
  (6 shorter events, 0.0 us)
Async XLA Ops:
  6.5 1.2 copy-start
  6.5 6.2 %copy-start.4 = (f32[256]{0:T(256)S(1)}, f32[256]{0:T(256)}, u32[]{:S(2)}) copy-start(f32[256]{0:T(256)} %param.9) | copy-start | bytes 3076
  6.5 6.2 %copy-start.3 = (f32[256,256]{1,0:T(8,128)S(1)}, f32[256,256]{1,0:T(8,128)}, u32[]{:S(2)}) copy-start(f32[256,256]{1,0:T(8,128)} %param.11) | copy-start | bytes 786436
  6.5 6.2 %copy-start.2 = (f32[256,256]{1,0:T(8,128)S(1)}, f32[256,256]{1,0:T(8,128)}, u32[]{:S(2)}) copy-start(f32[256,256]{1,0:T(8,128)} %param.8) | copy-start | bytes 786436
  6.5 155.0 %copy-start.1 = (f32[256,256]{1,0:T(8,128)S(1)}, f32[256,256]{1,0:T(8,128)}, u32[]{:S(2)}) copy-start(f32[256,256]{1,0:T(8,128)} %param.10) | copy-start | bytes 786436
  6.5 155.0 %all-reduce.3.cloned.1.call-start = ((), (), s32[]{:S(2)}) async-start(), calls=%async_computation | async-start | bytes 524288 | tf_op jit(solution)/shard_map/psum | solution.py:61
  12.7 211.3 %all-reduce.5.cloned.1.call-start = ((), (), s32[]{:S(2)}) async-start(), calls=%async_computation.1 | async-start | bytes 524288 | tf_op jit(solution)/shard_map/psum | solution.py:60
Sparse Core Ops, SparseCore 0:
  12.8 148.6 all-reduce.2
  163.9 60.0 all-reduce.4
